TPU v7x, 128 devices: a whole 4x4x4 slice. The times are simulated.
128 devices in a mesh: slab: 64 (over z, y, x), sub: 2 (over core).
Axes of the slice: x: 4, y: 4, z: 4, core: 2. Of those that a mesh axis runs over, the one named last changes fastest.
Arguments:
- part_cells: int32 [128, 128, 256], P(('slab', 'sub')), may hold values from 0 to 8191
- part_offsets: float32 [128, 128, 3, 256], P(('slab', 'sub')), may hold values from 0 to 1
- part_counts: int32 [128, 128], P(('slab', 'sub')), may hold values from 32 to 256, as said below
- w_first: bfloat16 [16, 27], replicated, may hold values from -1.25 to 1.25
- w_mid: bfloat16 [16, 432], replicated, may hold values from -0.3125 to 0.3125
- w_last: bfloat16 [16, 432], replicated, may hold values from -0.3125 to 0.3125
- w_head: bfloat16 [3, 32], replicated, may hold values from -1 to 1
- cotangent: bfloat16 [3, 256, 16, 256], P(None, 'slab', 'sub'), may hold values from -6 to 6
Outputs:
- force: bfloat16 [3, 256, 16, 256], P(None, 'slab', 'sub')
- grad_first: float32 [16, 27], replicated
- grad_mid: float32 [16, 432], replicated
- grad_last: float32 [16, 432], replicated
- grad_head: float32 [3, 32], replicated
Inputs may be any that keep to these rules, and one draw needn't show every extreme that they name: part_counts[s, d] is the number of used slots among the 256 slots from device s to brick d; one brick, drawn from the seed, gets 256 from every device. part_cells[s, d, k] is the cell (i * 8 + j) * 256 + l in brick d's own cells; slots at or above part_counts[s, d] are unused.
All inputs are finite; a program needn't handle non-finite values.
Results may differ from a plain program's by a relative error of at most 0.003.
The roundings to bfloat16 on the way count: a program that leaves them out, or rounds other values in their place, can miss the bound.
Values may be sent and summed in bfloat16 or wider, within the bound.
A program may use at most 192 MiB of HBM per device.

v0:
```python
import math
import jax
import jax.numpy as jnp
from jax import lax
from jax.sharding import PartitionSpec as P


def padded_2(x, sides, width):
    for axis, dim in sides:
        devices, length = (lax.axis_size(axis), x.shape[dim])
        up = [(i, (i + 1) % devices) for i in range(devices)]
        down = [(j, i) for i, j in up]
        last = lax.slice_in_dim(x, length - width, length, axis=dim)
        initial = lax.slice_in_dim(x, 0, width, axis=dim)
        before = lax.ppermute(last, axis, up)
        after = lax.ppermute(initial, axis, down)
        x = jnp.concatenate([before, x, after], axis=dim)
    return x


def passed_along(x, axis, by):
    devices = lax.axis_size(axis)
    return lax.ppermute(x, axis, [(i, (i + by) % devices) for i in range(devices)])


def silu_slope(value):
    sigma = jax.nn.sigmoid(value)
    return sigma * (1.0 + value * (1.0 - sigma))


def z_stack(plane):
    return jnp.concatenate([jnp.roll(plane, 1, axis=2), plane, jnp.roll(plane, -1, axis=2)], 0)


def conv_planes(padded, kernel, stacker):
    chans = padded.shape[0]
    out_x = padded.shape[1] - 2
    out_y = padded.shape[2] - 2
    out_chans = kernel.shape[0]
    blocks = kernel.reshape(out_chans, 3, 3, 3 * chans)
    stacks = [stacker(padded[:, plane]) for plane in range(out_x + 2)]
    depth_z = stacks[0].shape[2]
    results = []
    for plane in range(out_x):
        total = jnp.zeros((out_chans, out_y * depth_z), jnp.float32)
        for shift_x in range(3):
            for shift_y in range(3):
                piece = stacks[plane + shift_x][:, shift_y : shift_y + out_y].reshape(
                    3 * chans, out_y * depth_z
                )
                total = total + jnp.dot(
                    blocks[:, shift_x, shift_y], piece, preferred_element_type=jnp.float32
                )
        results.append(total.reshape(out_chans, out_y, depth_z))
    return jnp.stack(results, 1)


def weight_grad(padded, grad, stacker):
    chans = padded.shape[0]
    out_x = grad.shape[1]
    out_y = grad.shape[2]
    depth_z = grad.shape[3]
    out_chans = grad.shape[0]
    totals = [
        [jnp.zeros((out_chans, 3 * chans), jnp.float32) for shift_y in range(3)]
        for shift_x in range(3)
    ]
    for plane in range(out_x):
        grad_plane = grad[:, plane].reshape(out_chans, out_y * depth_z)
        for shift_x in range(3):
            stacked = stacker(padded[:, plane + shift_x])
            for shift_y in range(3):
                piece = stacked[:, shift_y : shift_y + out_y].reshape(3 * chans, out_y * depth_z)
                totals[shift_x][shift_y] = totals[shift_x][shift_y] + lax.dot_general(
                    grad_plane, piece, (((1,), (1,)), ((), ())), preferred_element_type=jnp.float32
                )
    joined = jnp.stack([jnp.stack(totals[shift_x], axis=1) for shift_x in range(3)], axis=1)
    return joined.reshape(out_chans, 27 * chans)


def flip_kernel(weights, chans):
    out_chans = weights.shape[0]
    shaped = weights.reshape(out_chans, 3, 3, 3, chans)[:, ::-1, ::-1, ::-1, :]
    return shaped.transpose(4, 1, 2, 3, 0).reshape(chans, 27 * out_chans)


def with_rims(field):
    return padded_2(field, (("slab", 1), ("sub", 2)), 1)


def finish(
    density_rim,
    pre_one,
    hidden_one,
    hidden_one_rim,
    pre_two,
    hidden_two_rim,
    w_mid,
    w_last,
    w_head,
    ct_field,
    rims,
    stacker,
):
    channels = w_mid.shape[0]
    extent = pre_one.shape[1:]
    pre_three = conv_planes(hidden_two_rim, w_last, stacker)
    hidden_three = jax.nn.silu(pre_three).astype(jnp.bfloat16)
    features = jnp.concatenate([hidden_three, hidden_one], 0).reshape(2 * channels, -1)
    ct_flat = ct_field.reshape(3, -1)
    force = jnp.dot(w_head, features, preferred_element_type=jnp.float32).astype(jnp.bfloat16)
    force = force.reshape((3,) + extent)
    grad_head = lax.dot_general(
        ct_flat, features, (((1,), (1,)), ((), ())), preferred_element_type=jnp.float32
    )
    back_features = jnp.dot(w_head.T, ct_flat, preferred_element_type=jnp.float32)
    grad_three = (back_features[:channels] * silu_slope(pre_three.reshape(channels, -1))).astype(
        jnp.bfloat16
    )
    grad_three = grad_three.reshape((channels,) + extent)
    grad_last = weight_grad(hidden_two_rim, grad_three, stacker)
    back_two = conv_planes(rims(grad_three), flip_kernel(w_last, channels), stacker)
    grad_two = (back_two * silu_slope(pre_two)).astype(jnp.bfloat16)
    grad_mid = weight_grad(hidden_one_rim, grad_two, stacker)
    back_one = conv_planes(rims(grad_two), flip_kernel(w_mid, channels), stacker)
    back_one = back_one + back_features[channels:].reshape((channels,) + extent)
    grad_one = (back_one * silu_slope(pre_one)).astype(jnp.bfloat16)
    grad_first = weight_grad(density_rim, grad_one, stacker)
    return (force, grad_first, grad_mid, grad_last, grad_head)


def per_device(part_cells, part_offsets, part_counts, w_first, w_mid, w_last, w_head, cotangent):
    n_slab = lax.axis_size("slab")
    n_sub = lax.axis_size("sub")
    width_x = cotangent.shape[1]
    width_y = cotangent.shape[2]
    depth_z = cotangent.shape[3]
    slot_cap = part_cells.shape[2]
    got_cells, got_offsets, got_counts = (
        lax.all_to_all(part_cells, ("slab", "sub"), split_axis=1, concat_axis=0, tiled=True),
        lax.all_to_all(part_offsets, ("slab", "sub"), split_axis=1, concat_axis=0, tiled=True),
        lax.all_to_all(part_counts, ("slab", "sub"), split_axis=1, concat_axis=0, tiled=True),
    )
    slot_cells = got_cells.reshape(-1, slot_cap)
    offsets = got_offsets.reshape(-1, 3, slot_cap)
    counts = got_counts.reshape(-1)
    slot_ids = jnp.arange(slot_cap, dtype=jnp.int32)
    live = (slot_ids[None, :] < counts[:, None]).astype(jnp.float32)
    cell_x = slot_cells // (width_y * depth_z)
    cell_y = slot_cells // depth_z % width_y
    cell_z = slot_cells % depth_z
    frac_x = offsets[:, 0]
    frac_y = offsets[:, 1]
    frac_z = offsets[:, 2]
    padded = jnp.zeros(((width_x + 1) * (width_y + 1) * depth_z,), jnp.float32)
    for corner_x in (0, 1):
        weight_x = frac_x if corner_x else 1.0 - frac_x
        for corner_y in (0, 1):
            weight_y = frac_y if corner_y else 1.0 - frac_y
            for corner_z in (0, 1):
                weight_z = frac_z if corner_z else 1.0 - frac_z
                share = live * weight_x * weight_y * weight_z
                index = ((cell_x + corner_x) * (width_y + 1) + cell_y + corner_y) * depth_z + (
                    cell_z + corner_z
                ) % depth_z
                padded = padded.at[index.reshape(-1)].add(share.reshape(-1))
    padded = padded.reshape(width_x + 1, width_y + 1, depth_z)
    from_below = passed_along(padded[width_x], "slab", 1)
    core = padded[:width_x].at[0].add(from_below)
    from_side = passed_along(core[:, width_y], "sub", 1)
    density = core[:, :width_y].at[:, 0].add(from_side)
    density_b = density.astype(jnp.bfloat16)[None]
    density_rim = with_rims(density_b)
    pre_one = conv_planes(density_rim, w_first, z_stack)
    hidden_one = jax.nn.silu(pre_one).astype(jnp.bfloat16)
    hidden_one_rim = with_rims(hidden_one)
    pre_two = conv_planes(hidden_one_rim, w_mid, z_stack)
    hidden_two = jax.nn.silu(pre_two).astype(jnp.bfloat16)
    hidden_two_rim = with_rims(hidden_two)
    force, grad_first, grad_mid, grad_last, grad_head = finish(
        density_rim,
        pre_one,
        hidden_one,
        hidden_one_rim,
        pre_two,
        hidden_two_rim,
        w_mid,
        w_last,
        w_head,
        cotangent,
        with_rims,
        z_stack,
    )
    sum_first, sum_mid, sum_last, sum_head = lax.psum(
        (grad_first, grad_mid, grad_last, grad_head), ("slab", "sub")
    )
    loss_scale = 1.0 / math.sqrt(width_x * n_slab * width_y * n_sub * depth_z)
    return (
        force,
        loss_scale * sum_first,
        loss_scale * sum_mid,
        loss_scale * sum_last,
        loss_scale * sum_head,
    )


def solution(mesh):
    in_specs = (
        P(("slab", "sub"), None, None),
        P(("slab", "sub"), None, None, None),
        P(("slab", "sub"), None),
        P(),
        P(),
        P(),
        P(),
        P(None, "slab", "sub", None),
    )
    out_specs = (P(None, "slab", "sub", None), P(), P(), P(), P())
    return jax.shard_map(
        per_device, mesh=mesh, in_specs=in_specs, out_specs=out_specs, check_vma=False
    )
```

profile of v0, /device:TPU:1, one launch (start us, length us, event | category | flops | bytes accessed | tf_op | source)
XLA Modules:
  0.0 1670.1 jit_solution(12769515616592546914)
XLA Ops:
  2.0 11.5 all-to-all-start.1
  17.3 5.9 all-to-all-done.1
  23.1 4.5 all-to-all-start
  27.6 2.4 reduce.4
  30.1 7.5 all-to-all-done
  37.7 4.2 all-to-all-start.2
  41.9 3.0 compare_select_fusion
  47.9 7.6 all-to-all-done.2
  56.8 171.0 %scatter_custom_fusion = f32[11520]{0:T(1024)S(1)} fusion(s32[32768]{0:T(1024)S(1)} %bitcast.1767, f32[32768]{0:T(1024)S(1)} %get-tuple-element.95, f32[]{:T(128)} %constant.137.clone.1), kind=kCustom, calls=%fused_computation.492 | custom fusion | flops 32768 | bytes 46084 | tf_op jit(solution)/shard_map/scatter-add | solution.py:166
  227.8 174.7 %scatter_fusion = f32[11520]{0:T(1024)S(1)} fusion(f32[11520]{0:T(1024)S(1)} %scatter_custom_fusion, s32[32768]{0:T(1024)S(1)} %bitcast.1646, f32[32768]{0:T(1024)S(1)} %get-tuple-element.94), kind=kCustom, calls=%fused_computation.1 | custom fusion | flops 32768 | bytes 524288 | tf_op jit(solution)/shard_map/scatter-add | solution.py:166
  402.5 174.9 %scatter_fusion.1 = f32[11520]{0:T(1024)S(1)} fusion(f32[11520]{0:T(1024)S(1)} %scatter_fusion, s32[32768]{0:T(1024)S(1)} %bitcast.1645, f32[32768]{0:T(1024)S(1)} %get-tuple-element.89), kind=kCustom, calls=%fused_computation.2 | custom fusion | flops 32768 | bytes 524288 | tf_op jit(solution)/shard_map/scatter-add | solution.py:166
  577.4 174.7 %scatter_fusion.2 = f32[11520]{0:T(1024)S(1)} fusion(f32[11520]{0:T(1024)S(1)} %scatter_fusion.1, s32[32768]{0:T(1024)S(1)} %bitcast.1643, f32[32768]{0:T(1024)S(1)} %copy-done.25), kind=kCustom, calls=%fused_computation.3 | custom fusion | flops 32768 | bytes 524288 | tf_op jit(solution)/shard_map/scatter-add | solution.py:166
  752.2 174.7 %scatter_fusion.3 = f32[11520]{0:T(1024)S(1)} fusion(f32[11520]{0:T(1024)S(1)} %scatter_fusion.2, s32[32768]{0:T(1024)S(1)} %bitcast.1644, f32[32768]{0:T(1024)S(1)} %copy-done.24), kind=kCustom, calls=%fused_computation.4 | custom fusion | flops 32768 | bytes 524288 | tf_op jit(solution)/shard_map/scatter-add | solution.py:166
  926.9 174.7 %scatter_fusion.4 = f32[11520]{0:T(1024)S(1)} fusion(f32[11520]{0:T(1024)S(1)} %scatter_fusion.3, s32[32768]{0:T(1024)S(1)} %bitcast.1642, f32[32768]{0:T(1024)S(1)} %copy-done.23), kind=kCustom, calls=%fused_computation.5 | custom fusion | flops 32768 | bytes 524288 | tf_op jit(solution)/shard_map/scatter-add | solution.py:166
  1101.7 174.7 %scatter_fusion.5 = f32[11520]{0:T(1024)S(1)} fusion(f32[11520]{0:T(1024)S(1)} %scatter_fusion.4, s32[32768]{0:T(1024)S(1)} %bitcast.1641, f32[32768]{0:T(1024)S(1)} %copy-done.22), kind=kCustom, calls=%fused_computation.6 | custom fusion | flops 32768 | bytes 524288 | tf_op jit(solution)/shard_map/scatter-add | solution.py:166
  1276.4 174.7 %scatter_fusion.6 = f32[11520]{0:T(1024)S(1)} fusion(f32[11520]{0:T(1024)S(1)} %scatter_fusion.5, s32[32768]{0:T(1024)S(1)} %bitcast.1640, f32[32768]{0:T(1024)S(1)} %copy-done.21), kind=kCustom, calls=%fused_computation.7 | custom fusion | flops 32768 | bytes 524288 | tf_op jit(solution)/shard_map/scatter-add | solution.py:166
  1451.3 8.0 collective-permute-done
  1462.4 6.9 collective-permute-start.3
  1483.7 7.2 collective-permute-start.7
  1506.3 7.0 collective-permute-start.11
  1552.9 3.6 collective-permute-done.14
  1575.0 2.5 collective-permute-start.19
  1582.4 3.7 collective-permute-done.18
  1604.5 62.7 %all-reduce = (f32[16,27]{0,1:T(8,128)S(1)}, f32[16,432]{1,0:T(8,128)S(1)}, f32[16,432]{1,0:T(8,128)S(1)}, f32[3,32]{1,0:T(4,128)S(1)}) all-reduce(f32[16,27]{0,1:T(8,128)S(1)} %reshape.1267, f32[16,432]{1,0:T(8,128)S(1)} %reshape.1268, f32[16,432]{1,0:T(8,128)S(1)} %reshape.1269, ...), channel_id=1, replica_groups=mesh['slab'=64,'sub'=2] {'slab','sub'}, use_global_device_ids=true, to_apply=%region_8.9 | all-reduce | flops 14352 | bytes 114816 | tf_op jit(solution)/shard_map/psum | solution.py:194
  (842 shorter events, 123.5 us)
Async XLA Ops:
  2.0 21.1 %all-to-all-start.1 = ((s32[1,128,1]{2,0,1:T(1,128)}), s32[1,128,1]{2,0,1:T(1,128)S(1)}, u32[]{:S(2)}, u32[]{:S(2)}) async-start(s32[1,128,1]{2,0,1:T(1,128)} %copy.241), calls=%async_computation.1 | async-start | bytes 131072 | tf_op jit(solution)/shard_map/all_to_all | solution.py:142
  23.1 14.5 all-to-all-start
  37.7 17.9 %all-to-all-start.2 = ((f32[1,128,3,256]{3,2,0,1:T(4,128)}), f32[1,128,3,256]{3,2,0,1:T(4,128)S(1)}, u32[]{:S(2)}, u32[]{:S(2)}) async-start(f32[1,128,3,256]{3,2,0,1:T(4,128)} %copy.242), calls=%async_computation.2 | async-start | bytes 1048576 | tf_op jit(solution)/shard_map/all_to_all | solution.py:141
  1451.2 8.1 collective-permute-start
  1459.3 2.9 collective-permute-start.1
  1462.3 8.0 collective-permute-start.2
  1462.4 7.9 collective-permute-start.3
  1470.3 2.4 collective-permute-start.4
  1471.8 1.6 collective-permute-start.5
  1483.7 9.6 collective-permute-start.6
  1483.7 9.6 collective-permute-start.7
  1493.3 1.6 collective-permute-start.8
  1506.3 23.2 %collective-permute-start.10 = (bf16[16,1,8,256]{3,0,2,1:T(8,128)(2,1)}, bf16[16,1,8,256]{3,0,2,1:T(8,128)(2,1)}, u32[]{:S(2)}, u32[]{:S(2)}) collective-permute-start(bf16[16,1,8,256]{3,0,2,1:T(8,128)(2,1)} %get-tuple-element.134), channel_id=1, source_target_pairs={{0,2},{2,4},{4,6},{6,8},{8,10},{10,12},{12,14},{14,16},{16,18},{18... | collective-permute-start | bytes 196616 | tf_op jit(solution)/shard_map/ppermute | solution.py:15
  1506.3 23.2 %collective-permute-start.11 = (bf16[16,1,8,256]{3,0,2,1:T(8,128)(2,1)}, bf16[16,1,8,256]{3,0,2,1:T(8,128)(2,1)}, u32[]{:S(2)}, u32[]{:S(2)}) collective-permute-start(bf16[16,1,8,256]{3,0,2,1:T(8,128)(2,1)} %get-tuple-element.135), channel_id=1, source_target_pairs={{2,0},{4,2},{6,4},{8,6},{10,8},{12,10},{14,12},{16,14},{18,16},{20... | collective-permute-start | bytes 196616 | tf_op jit(solution)/shard_map/ppermute | solution.py:16
  1530.3 1.6 collective-permute-start.12
  1531.0 1.4 collective-permute-start.13
  1546.0 10.5 collective-permute-start.15
  1547.9 8.6 collective-permute-start.14
  1557.4 3.5 collective-permute-start.16
  1559.0 2.0 collective-permute-start.17
  1575.0 7.4 collective-permute-start.19
  1577.5 8.6 collective-permute-start.18
  1586.1 2.9 collective-permute-start.20
  1588.1 1.5 collective-permute-start.21
  (71 other events, 3808.4 us)
where the time goes:
time: 1680 us; the launch traced here: 1670 us
  other arithmetic  1410 us (84%)
  blocking collectives  62.7 us (4%)
  starting transfers between devices  55.8 us (3%)
  matrix products  48.5 us (3%)
  waiting for transfers between devices  42.6 us (3%)
  local copies, waits for them, and re-layouts  42.4 us (3%)
    scatter-add x8, other arithmetic, per_device(): padded = padded.at[index.reshape(-1)].add(share.reshape(-1))  1390 us
    psum x1, blocking collectives, per_device(): lax.psum((grad_first, grad_mid, grad_last, grad_head), ('slab', 'sub'))  62.7 us
  transfers between devices with their start and end apart: 25, of which 17 were waited for; matrix products, arithmetic and copies ran while one was open for 3% of the time, Pallas kernels for 0%

commit v1 on v0

--- a/solution.py
+++ b/solution.py
@@ -192,7 +192,7 @@
         z_stack,
     )
     sum_first, sum_mid, sum_last, sum_head = lax.psum(
-        (grad_first, grad_mid, grad_last, grad_head), ("slab", "sub")
+        lax.psum((grad_first, grad_mid, grad_last, grad_head), "sub"), "slab"
     )
     loss_scale = 1.0 / math.sqrt(width_x * n_slab * width_y * n_sub * depth_z)
     return (

time: 1680 us -> 1960 us (1.17)
  the two profiles are of different devices: /device:TPU:1 before, /device:TPU:0 now
where the time goes in v1:
time: 1960 us; the launch traced here: 1950 us
  other arithmetic  1410 us (72%)
  blocking collectives  348 us (18%)
  starting transfers between devices  52.8 us (3%)
  matrix products  48.5 us (2%)
  waiting for transfers between devices  44.3 us (2%)
  local copies, waits for them, and re-layouts  42.4 us (2%)
    scatter-add x8, other arithmetic, per_device(): padded = padded.at[index.reshape(-1)].add(share.reshape(-1))  1390 us
    psum x1, blocking collectives, per_device(): lax.psum(lax.psum((grad_first, grad_mid, grad_last, grad_head), 'sub'), '...  344 us
  transfers between devices with their start and end apart: 25, of which 17 were waited for; matrix products, arithmetic and copies ran while one was open for 2% of the time, Pallas kernels for 0%

profile of v1, /device:TPU:0, one launch (start us, length us, event | category | flops | bytes accessed | tf_op | source)
XLA Modules:
  0.0 1954.2 jit_solution(7304304142221128079)
XLA Ops:
  2.0 11.1 all-to-all-start.1
  16.9 5.6 all-to-all-done.1
  22.5 4.8 all-to-all-start
  29.8 6.9 all-to-all-done
  36.7 4.8 all-to-all-start.2
  41.5 3.0 compare_select_fusion
  47.6 7.4 all-to-all-done.2
  56.3 171.0 %scatter_custom_fusion = f32[11520]{0:T(1024)S(1)} fusion(s32[32768]{0:T(1024)S(1)} %bitcast.1767, f32[32768]{0:T(1024)S(1)} %get-tuple-element.99, f32[]{:T(128)} %constant.137.clone.1), kind=kCustom, calls=%fused_computation.492 | custom fusion | flops 32768 | bytes 46084 | tf_op jit(solution)/shard_map/scatter-add | solution.py:166
  227.2 174.7 %scatter_fusion = f32[11520]{0:T(1024)S(1)} fusion(f32[11520]{0:T(1024)S(1)} %scatter_custom_fusion, s32[32768]{0:T(1024)S(1)} %bitcast.1646, f32[32768]{0:T(1024)S(1)} %get-tuple-element.98), kind=kCustom, calls=%fused_computation.1 | custom fusion | flops 32768 | bytes 524288 | tf_op jit(solution)/shard_map/scatter-add | solution.py:166
  402.0 174.9 %scatter_fusion.1 = f32[11520]{0:T(1024)S(1)} fusion(f32[11520]{0:T(1024)S(1)} %scatter_fusion, s32[32768]{0:T(1024)S(1)} %bitcast.1645, f32[32768]{0:T(1024)S(1)} %get-tuple-element.93), kind=kCustom, calls=%fused_computation.2 | custom fusion | flops 32768 | bytes 524288 | tf_op jit(solution)/shard_map/scatter-add | solution.py:166
  576.9 174.7 %scatter_fusion.2 = f32[11520]{0:T(1024)S(1)} fusion(f32[11520]{0:T(1024)S(1)} %scatter_fusion.1, s32[32768]{0:T(1024)S(1)} %bitcast.1643, f32[32768]{0:T(1024)S(1)} %copy-done.25), kind=kCustom, calls=%fused_computation.3 | custom fusion | flops 32768 | bytes 524288 | tf_op jit(solution)/shard_map/scatter-add | solution.py:166
  751.7 174.7 %scatter_fusion.3 = f32[11520]{0:T(1024)S(1)} fusion(f32[11520]{0:T(1024)S(1)} %scatter_fusion.2, s32[32768]{0:T(1024)S(1)} %bitcast.1644, f32[32768]{0:T(1024)S(1)} %copy-done.24), kind=kCustom, calls=%fused_computation.4 | custom fusion | flops 32768 | bytes 524288 | tf_op jit(solution)/shard_map/scatter-add | solution.py:166
  926.4 174.7 %scatter_fusion.4 = f32[11520]{0:T(1024)S(1)} fusion(f32[11520]{0:T(1024)S(1)} %scatter_fusion.3, s32[32768]{0:T(1024)S(1)} %bitcast.1642, f32[32768]{0:T(1024)S(1)} %copy-done.23), kind=kCustom, calls=%fused_computation.5 | custom fusion | flops 32768 | bytes 524288 | tf_op jit(solution)/shard_map/scatter-add | solution.py:166
  1101.2 174.7 %scatter_fusion.5 = f32[11520]{0:T(1024)S(1)} fusion(f32[11520]{0:T(1024)S(1)} %scatter_fusion.4, s32[32768]{0:T(1024)S(1)} %bitcast.1641, f32[32768]{0:T(1024)S(1)} %copy-done.22), kind=kCustom, calls=%fused_computation.6 | custom fusion | flops 32768 | bytes 524288 | tf_op jit(solution)/shard_map/scatter-add | solution.py:166
  1275.9 174.7 %scatter_fusion.6 = f32[11520]{0:T(1024)S(1)} fusion(f32[11520]{0:T(1024)S(1)} %scatter_fusion.5, s32[32768]{0:T(1024)S(1)} %bitcast.1640, f32[32768]{0:T(1024)S(1)} %copy-done.21), kind=kCustom, calls=%fused_computation.7 | custom fusion | flops 32768 | bytes 524288 | tf_op jit(solution)/shard_map/scatter-add | solution.py:166
  1451.3 8.6 collective-permute-done
  1461.3 7.4 collective-permute-start.3
  1482.5 7.5 collective-permute-start.7
  1505.0 7.5 collective-permute-start.11
  1552.1 4.6 collective-permute-done.14
  1574.0 2.7 collective-permute-start.19
  1581.8 4.8 collective-permute-done.18
  1603.2 3.9 all-reduce.1
  1607.1 344.1 %all-reduce = (f32[16,27]{0,1:T(8,128)S(1)}, f32[16,432]{1,0:T(8,128)S(1)}, f32[16,432]{1,0:T(8,128)S(1)}, f32[3,32]{1,0:T(4,128)S(1)}) all-reduce(f32[16,27]{0,1:T(8,128)S(1)} %get-tuple-element.48, f32[16,432]{1,0:T(8,128)S(1)} %get-tuple-element.49, ...), channel_id=1, replica_groups=mesh['slab'=64,'sub'=2] {'slab'}, use_global_device_ids=true, to_apply=%region_9.10 | all-reduce | flops 14352 | bytes 114816 | tf_op jit(solution)/shard_map/psum | solution.py:194
  (843 shorter events, 120.7 us)
Async XLA Ops:
  2.0 20.4 %all-to-all-start.1 = ((s32[1,128,1]{2,0,1:T(1,128)}), s32[1,128,1]{2,0,1:T(1,128)S(1)}, u32[]{:S(2)}, u32[]{:S(2)}) async-start(s32[1,128,1]{2,0,1:T(1,128)} %copy.241), calls=%async_computation.1 | async-start | bytes 131072 | tf_op jit(solution)/shard_map/all_to_all | solution.py:142
  22.5 14.2 all-to-all-start
  36.7 18.4 all-to-all-start.2
  1450.7 9.2 collective-permute-start
  1461.2 9.1 collective-permute-start.2
  1461.3 9.0 collective-permute-start.3
  1470.4 1.2 collective-permute-start.4
  1470.5 1.7 collective-permute-start.5
  1482.4 10.1 collective-permute-start.6
  1482.5 10.0 collective-permute-start.7
  1492.6 1.3 collective-permute-start.8
  1492.7 1.4 collective-permute-start.9
  1505.0 23.7 %collective-permute-start.10 = (bf16[16,1,8,256]{3,0,2,1:T(8,128)(2,1)}, bf16[16,1,8,256]{3,0,2,1:T(8,128)(2,1)}, u32[]{:S(2)}, u32[]{:S(2)}) collective-permute-start(bf16[16,1,8,256]{3,0,2,1:T(8,128)(2,1)} %get-tuple-element.138), channel_id=1, source_target_pairs={{0,2},{2,4},{4,6},{6,8},{8,10},{10,12},{12,14},{14,16},{16,18},{18... | collective-permute-start | bytes 196616 | tf_op jit(solution)/shard_map/ppermute | solution.py:15
  1505.0 23.7 %collective-permute-start.11 = (bf16[16,1,8,256]{3,0,2,1:T(8,128)(2,1)}, bf16[16,1,8,256]{3,0,2,1:T(8,128)(2,1)}, u32[]{:S(2)}, u32[]{:S(2)}) collective-permute-start(bf16[16,1,8,256]{3,0,2,1:T(8,128)(2,1)} %get-tuple-element.139), channel_id=1, source_target_pairs={{2,0},{4,2},{6,4},{8,6},{10,8},{12,10},{14,12},{16,14},{18,16},{20... | collective-permute-start | bytes 196616 | tf_op jit(solution)/shard_map/ppermute | solution.py:16
  1529.5 1.3 collective-permute-start.12
  1529.6 1.5 collective-permute-start.13
  1544.8 11.9 collective-permute-start.15
  1546.9 9.8 collective-permute-start.14
  1557.5 2.4 collective-permute-start.16
  1557.5 2.4 collective-permute-start.17
  1574.0 7.7 collective-permute-start.19
  1576.8 9.8 collective-permute-start.18
  1586.6 1.3 collective-permute-start.20
  1586.7 1.6 collective-permute-start.21
  (71 other events, 3808.3 us)
